TPU v7x, 128 devices: a whole 4x4x4 slice. The times are simulated.
128 devices in a mesh: tile: 8 (over z, core), lvl: 16 (over x, y).
Axes of the slice: x: 4, y: 4, z: 4, core: 2. Of those that a mesh axis runs over, the one named last changes fastest.
Arguments:
- parents: int32 [3, 1024, 4], P(None, ('tile', 'lvl')), may hold values from -1 to 3071, as said below
- factors: bfloat16 [3, 1024, 4, 256, 256], P(None, ('tile', 'lvl')), may hold values from -0.125 to 0.125
- chol: bfloat16 [4, 1024, 256, 256], P(None, ('tile', 'lvl')), as said below
- noise: bfloat16 [4, 1024, 256, 256], P(None, ('tile', 'lvl')), may hold values from -6 to 6
Outputs:
- samples: bfloat16 [4, 1024, 256, 256], P(None, ('tile', 'lvl'))
Inputs may be any that keep to these rules, and one draw needn't show every extreme that they name: `parents`: parents of a block of level s + 1 are blocks of levels 0 to s owned by a device of the same spatial tile or of the tile with index one less. Among the 32 entries of one device's blocks of one level, at most 2 name blocks owned by any one device of the same tile and at most 1 name blocks owned by any one device of the previous tile; in every draw, both bounds are reached by some device (devices of tile 0 have no previous tile, so their previous-tile entries are -1). `chol`: lower triangular with a positive diagonal.
All inputs are finite; a program needn't handle non-finite values.
Results may differ from a plain program's by a relative error of at most 0.0032.
Values may be sent and summed in bfloat16 or wider, within the bound.
A program may use at most 128 MiB of HBM per device.

v0:
```python
import jax
import jax.numpy as jnp
from jax import lax
from jax.sharding import PartitionSpec as P

NPAR = 4
CAP = 2
CAPX = 1


def passed_along(value, axis, steps):
    count = lax.axis_size(axis)
    first, last = (max(0, -steps), min(count, count - steps))
    return lax.ppermute(value, axis, [(source, source + steps) for source in range(first, last)])


def decode(block_ids, requester_tile, total_blocks, local_blocks, peer_count):
    is_valid = block_ids >= 0
    clipped = jnp.maximum(block_ids, 0)
    parent_level = clipped // total_blocks
    parent_block = clipped % total_blocks
    owner_dev = parent_block // local_blocks
    owner_tile = owner_dev // peer_count
    owner_lane = owner_dev % peer_count
    within = parent_block % local_blocks
    from_prior = owner_tile != requester_tile
    column = owner_lane + peer_count * from_prior.astype(jnp.int32)
    onehot = ((column[..., None] == jnp.arange(2 * peer_count)) & is_valid[..., None]).astype(
        jnp.int32
    )
    before = jnp.cumsum(onehot, axis=-2) - onehot
    slot_rank = jnp.sum(before * onehot, axis=-1)
    return (is_valid, parent_level * local_blocks + within, owner_lane, from_prior, slot_rank)


def slot_table(matched, source, slot_index, width):
    hits = matched[..., None] & (slot_index[..., None] == jnp.arange(width))
    return jnp.sum(jnp.where(hits, source[..., None] + 1, 0), axis=1) - 1


def fill_slots(held_blocks, picked):
    rows = held_blocks[jnp.maximum(picked, 0)]
    return jnp.where((picked >= 0)[..., None, None], rows, jnp.zeros((), rows.dtype))


def noise_part(lower, draws):
    return jnp.einsum("kij,kjr->kir", lower, draws, preferred_element_type=jnp.float32)


def shards(parents, factors, chol, noise):
    peer_count = lax.axis_size("lvl")
    tile_count = lax.axis_size("tile")
    own_lane = lax.axis_index("lvl")
    own_tile = lax.axis_index("tile")
    depth = chol.shape[0]
    local_blocks = chol.shape[1]
    block_rows = chol.shape[2]
    realize = noise.shape[3]
    total_blocks = local_blocks * peer_count * tile_count
    refs_dev = local_blocks * NPAR
    gathered = lax.all_gather(parents, "lvl", axis=1, tiled=True).reshape(
        depth - 1, peer_count, refs_dev
    )
    held_blocks = jnp.zeros(((2 * depth - 1) * local_blocks, block_rows, realize), jnp.bfloat16)
    following = passed_along(gathered, "tile", -1)
    following = jnp.where(own_tile + 1 < tile_count, following, -1)
    latest = noise_part(chol[0], noise[0]).astype(jnp.bfloat16)
    held_blocks = held_blocks.at[0:local_blocks].set(latest)
    outputs = [latest]
    for section in range(1, depth):
        mine_valid, mine_source, mine_lane, mine_prior, mine_rank = decode(
            parents[section - 1].reshape(refs_dev), own_tile, total_blocks, local_blocks, peer_count
        )
        is_valid, source, owner_lane, from_prior, slot_rank = decode(
            gathered[section - 1], own_tile, total_blocks, local_blocks, peer_count
        )
        matched = is_valid & jnp.logical_not(from_prior) & (owner_lane == own_lane)
        same_sent = fill_slots(held_blocks, slot_table(matched, source, slot_rank, CAP))
        same_got = lax.all_to_all(same_sent, "lvl", split_axis=0, concat_axis=0, tiled=True)
        next_valid, next_source, next_lane, next_prior, next_rank = decode(
            following[section - 1], own_tile + 1, total_blocks, local_blocks, peer_count
        )
        next_match = next_valid & next_prior & (next_lane == own_lane)
        prior_sent = fill_slots(held_blocks, slot_table(next_match, next_source, next_rank, CAPX))
        spread = lax.all_to_all(prior_sent, "lvl", split_axis=0, concat_axis=0, tiled=True)
        crossed = passed_along(spread, "tile", 1)
        same_vals = same_got.reshape(-1, block_rows, realize)[
            mine_lane * CAP + jnp.minimum(mine_rank, CAP - 1)
        ]
        prior_vals = crossed.reshape(-1, block_rows, realize)[
            mine_lane * CAPX + jnp.minimum(mine_rank, CAPX - 1)
        ]
        parent_vals = jnp.where(mine_prior[:, None, None], prior_vals, same_vals)
        parent_vals = jnp.where(
            mine_valid[:, None, None], parent_vals, jnp.zeros((), parent_vals.dtype)
        )
        parent_vals = parent_vals.reshape(local_blocks, NPAR, block_rows, realize)
        mixed = jnp.einsum(
            "ksij,ksjr->kir", factors[section - 1], parent_vals, preferred_element_type=jnp.float32
        )
        latest = (mixed + noise_part(chol[section], noise[section])).astype(jnp.bfloat16)
        held_blocks = held_blocks.at[section * local_blocks : (section + 1) * local_blocks].set(
            latest
        )
        outputs.append(latest)
    return jnp.stack(outputs)


def solution(mesh):
    placed = (
        P(None, ("tile", "lvl"), None),
        P(None, ("tile", "lvl"), None, None, None),
        P(None, ("tile", "lvl"), None, None),
        P(None, ("tile", "lvl"), None, None),
    )
    return jax.shard_map(
        shards,
        mesh=mesh,
        in_specs=placed,
        out_specs=P(None, ("tile", "lvl"), None, None),
        check_vma=False,
    )
```

profile of v0, /device:TPU:16, one launch (start us, length us, event | category | flops | bytes accessed | tf_op | source)
XLA Modules:
  0.0 435.5 jit_solution(4157353875013559059)
XLA Ops:
  0.8 23.4 %all_gather.3 = s32[3,128,4]{2,0,1:T(4,128)S(1)} all-gather(s32[3,8,4]{2,0,1:T(4,128)S(1)} %copy.149), channel_id=1, replica_groups=mesh['tile'=8,'lvl'=16] {'lvl'}, dimensions={1}, use_global_device_ids=true | all-gather | bytes 6528 | tf_op jit(solution)/shard_map/all_gather | solution.py:61
  25.7 2.0 convolution_convert_fusion
  27.7 1.8 and_reduce_fusion
  30.5 3.8 scatter.10
  39.4 3.9 gather_fusion
  43.3 2.3 fusion.26
  45.5 5.8 %all-to-all-start = ((bf16[16,1,256,256]{3,2,1,0:T(8,128)(2,1)}), bf16[16,1,256,256]{3,2,1,0:T(8,128)(2,1)S(1)}, u32[]{:S(2)}, u32[]{:S(2)}) async-start(bf16[16,1,256,256]{3,2,1,0:T(8,128)(2,1)} %fusion.26), calls=%async_computation | async-start | bytes 4194304 | tf_op jit(solution)/shard_map/all_to_all | solution.py:85
  51.3 2.2 compare_reduce_fusion.1
  57.7 5.9 %gather_fusion.2 = bf16[32,256,256]{2,1,0:T(8,128)(2,1)} fusion(bf16[56,256,256]{2,1,0:T(8,128)(2,1)} %scatter.10, s32[1024]{0:T(1024)S(1)} %pad_clamp_fusion.9), kind=kCustom, calls=%fused_computation.2 | custom fusion | bytes 8388736 | tf_op jit(solution)/shard_map/gather | solution.py:42
  63.7 4.5 %broadcast_select_fusion.2 = bf16[16,2,256,256]{3,2,1,0:T(8,128)(2,1)} fusion(bf16[16,2,256,256]{3,2,1,0:T(8,128)(2,1)} %bitcast.301, pred[16,2]{1,0:T(8,128)(4,1)S(1)} %copy.168), kind=kLoop, calls=%fused_computation.34 | loop fusion | flops 2097152 | bytes 8388640 | tf_op jit(solution)/shard_map/jit(_where)/select_n | solution.py:43
  68.3 13.8 %all-to-all-done = bf16[16,1,256,256]{3,2,1,0:T(8,128)(2,1)S(1)} async-done(((bf16[16,1,256,256]{3,2,1,0:T(8,128)(2,1)}), bf16[16,1,256,256]{3,2,1,0:T(8,128)(2,1)S(1)}, u32[]{:S(2)}, u32[]{:S(2)}) %all-to-all-start) | async-done | bytes 2097184 | tf_op jit(solution)/shard_map/all_to_all | solution.py:85
  82.0 7.4 %all-to-all-start.1 = ((bf16[16,2,256,256]{3,2,1,0:T(8,128)(2,1)}), bf16[16,2,256,256]{3,2,1,0:T(8,128)(2,1)}, u32[]{:S(2)}, u32[]{:S(2)}) async-start(bf16[16,2,256,256]{3,2,1,0:T(8,128)(2,1)} %broadcast_select_fusion.2), calls=%async_computation.1 | async-start | bytes 8388608 | tf_op jit(solution)/shard_map/all_to_all | solution.py:79
  90.3 1.6 collective-permute-start.1
  92.4 3.3 fusion.59
  95.7 50.1 %all-to-all-done.1 = bf16[16,2,256,256]{3,2,1,0:T(8,128)(2,1)} async-done(((bf16[16,2,256,256]{3,2,1,0:T(8,128)(2,1)}), bf16[16,2,256,256]{3,2,1,0:T(8,128)(2,1)}, u32[]{:S(2)}, u32[]{:S(2)}) %all-to-all-start.1) | async-done | bytes 4194336 | tf_op jit(solution)/shard_map/all_to_all | solution.py:79
  145.7 5.0 %gather_fusion.3 = bf16[32,256,256]{2,1,0:T(8,128)(2,1)} fusion(bf16[32,256,256]{2,1,0:T(8,128)(2,1)} %bitcast.19, s32[1024]{0:T(1024)S(1)} %pad_clamp_fusion.8), kind=kCustom, calls=%fused_computation.3 | custom fusion | bytes 8388736 | tf_op jit(solution)/shard_map/gather | solution.py:87
  150.7 6.5 %copy.171 = bf16[8,4,256,256]{2,3,1,0:T(8,128)(2,1)} copy(bf16[8,4,256,256]{3,2,1,0:T(8,128)(2,1)} %bitcast.304) | data formatting | bytes 8388608 | tf_op jit(solution)/shard_map/gather | solution.py:87
  157.2 2.8 gather_fusion.1
  160.0 6.6 %copy.170 = bf16[8,4,256,256]{2,3,1,0:T(8,128)(2,1)} copy(bf16[8,4,256,256]{3,2,1,0:T(8,128)(2,1)} %bitcast.305) | data formatting | bytes 8388608 | tf_op jit(solution)/shard_map/gather | solution.py:90
  166.6 7.7 %constant_dynamic-update-slice_fusion.1 = (bf16[56,256,256]{2,1,0:T(8,128)(2,1)}, bf16[8,256,256]{2,1,0:T(8,128)(2,1)}) fusion(bf16[56,256,256]{2,1,0:T(8,128)(2,1)} %scatter.10, f32[8,256,256]{2,1,0:T(8,128)S(1)} %copy-done.4, bf16[3,8,4,256,256]{4,3,2,1,0:T(8,128)(2,1)} %param.11, bf16[8,4,256,256]{2,3,1,0:T(8,128)(2,1)} %copy.170, ...), kind=kOutput, calls=%fused_computation.555 | convolution fusion | flops 1078984704 | bytes 16777280 | tf_op jit(solution)/shard_map/ksij,ksjr->kir/dot_general | solution.py:98
  174.3 3.8 gather_fusion.4
  179.8 18.0 %all-to-all-start.2 = ((bf16[16,1,256,256]{3,2,1,0:T(8,128)(2,1)}), bf16[16,1,256,256]{3,2,1,0:T(8,128)(2,1)S(1)}, u32[]{:S(2)}, u32[]{:S(2)}) async-start(bf16[16,1,256,256]{3,2,1,0:T(8,128)(2,1)} %fusion.25), calls=%async_computation.2 | async-start | bytes 4194304 | tf_op jit(solution)/shard_map/all_to_all | solution.py:85
  201.1 5.9 %gather_fusion.6 = bf16[32,256,256]{2,1,0:T(8,128)(2,1)} fusion(bf16[56,256,256]{2,1,0:T(8,128)(2,1)} %get-tuple-element.83, s32[1024]{0:T(1024)S(1)} %pad_clamp_fusion.5), kind=kCustom, calls=%fused_computation.6 | custom fusion | bytes 8388736 | tf_op jit(solution)/shard_map/gather | solution.py:42
  207.0 4.5 %broadcast_select_fusion.1 = bf16[16,2,256,256]{3,2,1,0:T(8,128)(2,1)} fusion(bf16[16,2,256,256]{3,2,1,0:T(8,128)(2,1)} %bitcast.303, pred[16,2]{1,0:T(8,128)(4,1)S(1)} %copy.191), kind=kLoop, calls=%fused_computation.31 | loop fusion | flops 2097152 | bytes 8388640 | tf_op jit(solution)/shard_map/jit(_where)/select_n | solution.py:43
  211.6 12.0 %all-to-all-done.2 = bf16[16,1,256,256]{3,2,1,0:T(8,128)(2,1)S(1)} async-done(((bf16[16,1,256,256]{3,2,1,0:T(8,128)(2,1)}), bf16[16,1,256,256]{3,2,1,0:T(8,128)(2,1)S(1)}, u32[]{:S(2)}, u32[]{:S(2)}) %all-to-all-start.2) | async-done | bytes 2097184 | tf_op jit(solution)/shard_map/all_to_all | solution.py:85
  225.0 7.1 %all-to-all-start.3 = ((bf16[16,2,256,256]{3,2,1,0:T(8,128)(2,1)}), bf16[16,2,256,256]{3,2,1,0:T(8,128)(2,1)}, u32[]{:S(2)}, u32[]{:S(2)}) async-start(bf16[16,2,256,256]{3,2,1,0:T(8,128)(2,1)} %broadcast_select_fusion.1), calls=%async_computation.3 | async-start | bytes 8388608 | tf_op jit(solution)/shard_map/all_to_all | solution.py:79
  234.4 3.3 fusion.56
  237.7 44.6 %all-to-all-done.3 = bf16[16,2,256,256]{3,2,1,0:T(8,128)(2,1)} async-done(((bf16[16,2,256,256]{3,2,1,0:T(8,128)(2,1)}), bf16[16,2,256,256]{3,2,1,0:T(8,128)(2,1)}, u32[]{:S(2)}, u32[]{:S(2)}) %all-to-all-start.3) | async-done | bytes 4194336 | tf_op jit(solution)/shard_map/all_to_all | solution.py:79
  282.3 5.0 %gather_fusion.7 = bf16[32,256,256]{2,1,0:T(8,128)(2,1)} fusion(bf16[32,256,256]{2,1,0:T(8,128)(2,1)} %bitcast.45, s32[1024]{0:T(1024)S(1)} %pad_clamp_fusion.4), kind=kCustom, calls=%fused_computation.7 | custom fusion | bytes 8388736 | tf_op jit(solution)/shard_map/gather | solution.py:87
  287.3 6.5 %copy.194 = bf16[8,4,256,256]{2,3,1,0:T(8,128)(2,1)} copy(bf16[8,4,256,256]{3,2,1,0:T(8,128)(2,1)} %bitcast.306) | data formatting | bytes 8388608 | tf_op jit(solution)/shard_map/gather | solution.py:87
  293.8 2.8 gather_fusion.5
  296.6 6.6 %copy.193 = bf16[8,4,256,256]{2,3,1,0:T(8,128)(2,1)} copy(bf16[8,4,256,256]{3,2,1,0:T(8,128)(2,1)} %bitcast.307) | data formatting | bytes 8388608 | tf_op jit(solution)/shard_map/gather | solution.py:90
  303.2 7.6 %constant_dynamic-update-slice_fusion = (bf16[56,256,256]{2,1,0:T(8,128)(2,1)}, bf16[8,256,256]{2,1,0:T(8,128)(2,1)}) fusion(bf16[56,256,256]{2,1,0:T(8,128)(2,1)} %get-tuple-element.83, f32[8,256,256]{2,1,0:T(8,128)S(1)} %copy-done.3, bf16[3,8,4,256,256]{4,3,2,1,0:T(8,128)(2,1)} %param.11, bf16[8,4,256,256]{2,3,1,0:T(8,128)(2,1)} %copy.193, ...), kind=kOutput, calls=%fused_computation.554 | convolution fusion | flops 1078984704 | bytes 16777280 | tf_op jit(solution)/shard_map/ksij,ksjr->kir/dot_general | solution.py:98
  310.8 3.8 gather_fusion.8
  314.5 1.6 fusion.24
  316.1 6.3 %all-to-all-start.4 = ((bf16[16,1,256,256]{3,2,1,0:T(8,128)(2,1)}), bf16[16,1,256,256]{3,2,1,0:T(8,128)(2,1)S(1)}, u32[]{:S(2)}, u32[]{:S(2)}) async-start(bf16[16,1,256,256]{3,2,1,0:T(8,128)(2,1)} %fusion.24), calls=%async_computation.4 | async-start | bytes 4194304 | tf_op jit(solution)/shard_map/all_to_all | solution.py:85
  324.2 5.9 %gather_fusion.10 = bf16[32,256,256]{2,1,0:T(8,128)(2,1)} fusion(bf16[56,256,256]{2,1,0:T(8,128)(2,1)} %get-tuple-element.85, s32[1024]{0:T(1024)S(1)} %pad_clamp_fusion.1), kind=kCustom, calls=%fused_computation.10 | custom fusion | bytes 8388736 | tf_op jit(solution)/shard_map/gather | solution.py:42
  330.1 4.5 %broadcast_select_fusion = bf16[16,2,256,256]{3,2,1,0:T(8,128)(2,1)} fusion(bf16[16,2,256,256]{3,2,1,0:T(8,128)(2,1)} %bitcast.302, pred[16,2]{1,0:T(8,128)(4,1)S(1)} %copy.214), kind=kLoop, calls=%fused_computation.28 | loop fusion | flops 2097152 | bytes 8388640 | tf_op jit(solution)/shard_map/jit(_where)/select_n | solution.py:43
  334.6 12.8 %all-to-all-done.4 = bf16[16,1,256,256]{3,2,1,0:T(8,128)(2,1)S(1)} async-done(((bf16[16,1,256,256]{3,2,1,0:T(8,128)(2,1)}), bf16[16,1,256,256]{3,2,1,0:T(8,128)(2,1)S(1)}, u32[]{:S(2)}, u32[]{:S(2)}) %all-to-all-start.4) | async-done | bytes 2097184 | tf_op jit(solution)/shard_map/all_to_all | solution.py:85
  348.8 6.9 %all-to-all-start.5 = ((bf16[16,2,256,256]{3,2,1,0:T(8,128)(2,1)}), bf16[16,2,256,256]{3,2,1,0:T(8,128)(2,1)}, u32[]{:S(2)}, u32[]{:S(2)}) async-start(bf16[16,2,256,256]{3,2,1,0:T(8,128)(2,1)} %broadcast_select_fusion), calls=%async_computation.5 | async-start | bytes 8388608 | tf_op jit(solution)/shard_map/all_to_all | solution.py:79
  358.1 3.4 fusion.53
  361.5 44.4 %all-to-all-done.5 = bf16[16,2,256,256]{3,2,1,0:T(8,128)(2,1)} async-done(((bf16[16,2,256,256]{3,2,1,0:T(8,128)(2,1)}), bf16[16,2,256,256]{3,2,1,0:T(8,128)(2,1)}, u32[]{:S(2)}, u32[]{:S(2)}) %all-to-all-start.5) | async-done | bytes 4194336 | tf_op jit(solution)/shard_map/all_to_all | solution.py:79
  406.0 5.0 %gather_fusion.11 = bf16[32,256,256]{2,1,0:T(8,128)(2,1)} fusion(bf16[32,256,256]{2,1,0:T(8,128)(2,1)} %bitcast.71, s32[1024]{0:T(1024)S(1)} %pad_clamp_fusion), kind=kCustom, calls=%fused_computation.11 | custom fusion | bytes 8388736 | tf_op jit(solution)/shard_map/gather | solution.py:87
  411.0 6.4 %copy.217 = bf16[8,4,256,256]{2,3,1,0:T(8,128)(2,1)} copy(bf16[8,4,256,256]{3,2,1,0:T(8,128)(2,1)} %bitcast.308) | data formatting | bytes 8388608 | tf_op jit(solution)/shard_map/gather | solution.py:87
  417.4 2.8 gather_fusion.9
  420.3 6.6 %copy.216 = bf16[8,4,256,256]{2,3,1,0:T(8,128)(2,1)} copy(bf16[8,4,256,256]{3,2,1,0:T(8,128)(2,1)} %bitcast.309) | data formatting | bytes 8388608 | tf_op jit(solution)/shard_map/gather | solution.py:90
  426.9 6.4 %fusion.42 = bf16[1,8,256,256]{3,2,1,0:T(8,128)(2,1)S(1)} fusion(f32[8,256,256]{2,1,0:T(8,128)S(1)} %copy-done.5, bf16[3,8,4,256,256]{4,3,2,1,0:T(8,128)(2,1)} %param.11, bf16[8,4,256,256]{2,3,1,0:T(8,128)(2,1)} %copy.216, bf16[8,4,256,256]{2,3,1,0:T(8,128)(2,1)} %copy.217, pred[8,4]{1,0:T(8,128)(4,1)S(1)} %copy.197, pred[8,4]{1,0:T(8,128)(4,1)S(1)} %copy.196), kind=kOutput, calls=%fused_computation.53 | convolution fusion | flops 1078984704 | bytes 15728704 | tf_op jit(solution)/shard_map/ksij,ksjr->kir/dot_general | solution.py:98
  433.3 2.3 pad_maximum_fusion
  (170 shorter events, 27.8 us)
Async XLA Ops:
  24.4 9.8 %collective-permute-start = (s32[3,16,32]{1,2,0:T(8,128)S(1)}, s32[3,16,32]{1,2,0:T(8,128)S(1)}, u32[]{:S(2)}, u32[]{:S(2)}) collective-permute-start(s32[3,16,32]{1,2,0:T(8,128)S(1)} %copy.151), channel_id=1, source_target_pairs={{16,0},{32,16},{48,32},{64,48},{80,64},{96,80},{112,96},{17,1},{33... | collective-permute-start | bytes 18440 | tf_op jit(solution)/shard_map/ppermute | solution.py:14
  45.5 36.5 %all-to-all-start = ((bf16[16,1,256,256]{3,2,1,0:T(8,128)(2,1)}), bf16[16,1,256,256]{3,2,1,0:T(8,128)(2,1)S(1)}, u32[]{:S(2)}, u32[]{:S(2)}) async-start(bf16[16,1,256,256]{3,2,1,0:T(8,128)(2,1)} %fusion.26), calls=%async_computation | async-start | bytes 4194304 | tf_op jit(solution)/shard_map/all_to_all | solution.py:85
  68.3 21.1 %copy-start.10 = (s32[3,8,4]{1,2,0:T(4,128)S(1)}, s32[3,8,4]{1,2,0:T(4,128)}, u32[]{:S(2)}) copy-start(s32[3,8,4]{1,2,0:T(4,128)} %param.10) | copy-start | bytes 1156
  82.0 7.4 %copy-start.1 = (bf16[16,1,256,256]{3,2,1,0:T(8,128)(2,1)}, bf16[16,1,256,256]{3,2,1,0:T(8,128)(2,1)S(1)}, u32[]{:S(2)}) copy-start(bf16[16,1,256,256]{3,2,1,0:T(8,128)(2,1)S(1)} %all-to-all-done) | copy-start | bytes 6291460
  82.0 63.7 %all-to-all-start.1 = ((bf16[16,2,256,256]{3,2,1,0:T(8,128)(2,1)}), bf16[16,2,256,256]{3,2,1,0:T(8,128)(2,1)}, u32[]{:S(2)}, u32[]{:S(2)}) async-start(bf16[16,2,256,256]{3,2,1,0:T(8,128)(2,1)} %broadcast_select_fusion.2), calls=%async_computation.1 | async-start | bytes 8388608 | tf_op jit(solution)/shard_map/all_to_all | solution.py:79
  89.4 6.2 %copy-start.16 = (s32[16]{0:T(128)S(1)}, s32[16]{0:T(128)}, u32[]{:S(2)}) copy-start(s32[16]{0:T(128)} %get-tuple-element.54) | copy-start | bytes 196
  90.3 66.9 %collective-permute-start.1 = (bf16[16,1,256,256]{3,2,1,0:T(8,128)(2,1)}, bf16[16,1,256,256]{3,2,1,0:T(8,128)(2,1)S(1)}, u32[]{:S(2)}, u32[]{:S(2)}) collective-permute-start(bf16[16,1,256,256]{3,2,1,0:T(8,128)(2,1)} %copy-done.1), channel_id=1, source_target_pairs={{0,16},{16,32},{32,48},{48,64},{64,80},{80,96},{96,112},{1,17},{17... | collective-permute-start | bytes 6291464 | tf_op jit(solution)/shard_map/ppermute | solution.py:14
  160.0 6.6 %copy-start.4 = (f32[8,256,256]{2,1,0:T(8,128)S(1)}, f32[8,256,256]{2,1,0:T(8,128)}, u32[]{:S(2)}) copy-start(f32[8,256,256]{2,1,0:T(8,128)} %fusion.59) | copy-start | bytes 6291460
  178.1 19.7 %copy-start.9 = (s32[128,4]{1,0:T(8,128)S(1)}, s32[128,4]{1,0:T(8,128)}, u32[]{:S(2)}) copy-start(s32[128,4]{1,0:T(8,128)} %get-tuple-element.52) | copy-start | bytes 6148
  178.1 19.8 %copy-start.8 = (s32[128,4]{1,0:T(8,128)S(1)}, s32[128,4]{1,0:T(8,128)}, u32[]{:S(2)}) copy-start(s32[128,4]{1,0:T(8,128)} %get-tuple-element.47) | copy-start | bytes 6148
  178.1 20.3 %copy-start.14 = (pred[128,4]{1,0:T(8,128)(4,1)S(1)}, pred[128,4]{1,0:T(8,128)(4,1)}, u32[]{:S(2)}) copy-start(pred[128,4]{1,0:T(8,128)(4,1)} %get-tuple-element.43) | copy-start | bytes 1540
  178.1 20.5 %copy-start.13 = (pred[128,4]{1,0:T(8,128)(4,1)S(1)}, pred[128,4]{1,0:T(8,128)(4,1)}, u32[]{:S(2)}) copy-start(pred[128,4]{1,0:T(8,128)(4,1)} %get-tuple-element.42) | copy-start | bytes 1540
  178.1 20.7 %copy-start.12 = (pred[128,4]{1,0:T(8,128)(4,1)S(1)}, pred[128,4]{1,0:T(8,128)(4,1)}, u32[]{:S(2)}) copy-start(pred[128,4]{1,0:T(8,128)(4,1)} %get-tuple-element.45) | copy-start | bytes 1540
  178.2 22.2 %copy-start.11 = (pred[128,4]{1,0:T(8,128)(4,1)S(1)}, pred[128,4]{1,0:T(8,128)(4,1)}, u32[]{:S(2)}) copy-start(pred[128,4]{1,0:T(8,128)(4,1)} %get-tuple-element.41) | copy-start | bytes 1540
  179.8 43.8 %all-to-all-start.2 = ((bf16[16,1,256,256]{3,2,1,0:T(8,128)(2,1)}), bf16[16,1,256,256]{3,2,1,0:T(8,128)(2,1)S(1)}, u32[]{:S(2)}, u32[]{:S(2)}) async-start(bf16[16,1,256,256]{3,2,1,0:T(8,128)(2,1)} %fusion.25), calls=%async_computation.2 | async-start | bytes 4194304 | tf_op jit(solution)/shard_map/all_to_all | solution.py:85
  223.6 1.4 copy-start
  225.0 57.3 %all-to-all-start.3 = ((bf16[16,2,256,256]{3,2,1,0:T(8,128)(2,1)}), bf16[16,2,256,256]{3,2,1,0:T(8,128)(2,1)}, u32[]{:S(2)}, u32[]{:S(2)}) async-start(bf16[16,2,256,256]{3,2,1,0:T(8,128)(2,1)} %broadcast_select_fusion.1), calls=%async_computation.3 | async-start | bytes 8388608 | tf_op jit(solution)/shard_map/all_to_all | solution.py:79
  232.1 5.6 %copy-start.15 = (s32[16]{0:T(128)S(1)}, s32[16]{0:T(128)}, u32[]{:S(2)}) copy-start(s32[16]{0:T(128)} %get-tuple-element.53) | copy-start | bytes 196
  232.1 61.7 %collective-permute-start.2 = (bf16[16,1,256,256]{3,2,1,0:T(8,128)(2,1)}, bf16[16,1,256,256]{3,2,1,0:T(8,128)(2,1)S(1)}, u32[]{:S(2)}, u32[]{:S(2)}) collective-permute-start(bf16[16,1,256,256]{3,2,1,0:T(8,128)(2,1)} %copy-done), channel_id=1, source_target_pairs={{0,16},{16,32},{32,48},{48,64},{64,80},{80,96},{96,112},{1,17},{17... | collective-permute-start | bytes 6291464 | tf_op jit(solution)/shard_map/ppermute | solution.py:14
  296.6 6.6 %copy-start.3 = (f32[8,256,256]{2,1,0:T(8,128)S(1)}, f32[8,256,256]{2,1,0:T(8,128)}, u32[]{:S(2)}) copy-start(f32[8,256,256]{2,1,0:T(8,128)} %fusion.56) | copy-start | bytes 6291460
  316.1 31.3 %all-to-all-start.4 = ((bf16[16,1,256,256]{3,2,1,0:T(8,128)(2,1)}), bf16[16,1,256,256]{3,2,1,0:T(8,128)(2,1)S(1)}, u32[]{:S(2)}, u32[]{:S(2)}) async-start(bf16[16,1,256,256]{3,2,1,0:T(8,128)(2,1)} %fusion.24), calls=%async_computation.4 | async-start | bytes 4194304 | tf_op jit(solution)/shard_map/all_to_all | solution.py:85
  347.5 1.3 copy-start.2
  348.8 57.2 %all-to-all-start.5 = ((bf16[16,2,256,256]{3,2,1,0:T(8,128)(2,1)}), bf16[16,2,256,256]{3,2,1,0:T(8,128)(2,1)}, u32[]{:S(2)}, u32[]{:S(2)}) async-start(bf16[16,2,256,256]{3,2,1,0:T(8,128)(2,1)} %broadcast_select_fusion), calls=%async_computation.5 | async-start | bytes 8388608 | tf_op jit(solution)/shard_map/all_to_all | solution.py:79
  355.7 61.7 %collective-permute-start.3 = (bf16[16,1,256,256]{3,2,1,0:T(8,128)(2,1)}, bf16[16,1,256,256]{3,2,1,0:T(8,128)(2,1)S(1)}, u32[]{:S(2)}, u32[]{:S(2)}) collective-permute-start(bf16[16,1,256,256]{3,2,1,0:T(8,128)(2,1)} %copy-done.2), channel_id=1, source_target_pairs={{0,16},{16,32},{32,48},{48,64},{64,80},{80,96},{96,112},{1,17},{17... | collective-permute-start | bytes 6291464 | tf_op jit(solution)/shard_map/ppermute | solution.py:14
  420.3 6.6 %copy-start.5 = (f32[8,256,256]{2,1,0:T(8,128)S(1)}, f32[8,256,256]{2,1,0:T(8,128)}, u32[]{:S(2)}) copy-start(f32[8,256,256]{2,1,0:T(8,128)} %fusion.53) | copy-start | bytes 6291460
  426.9 6.4 %copy-start.6 = (bf16[8,256,256]{2,1,0:T(8,128)(2,1)S(1)}, bf16[8,256,256]{2,1,0:T(8,128)(2,1)}, u32[]{:S(2)}) copy-start(bf16[8,256,256]{2,1,0:T(8,128)(2,1)} %get-tuple-element.84) | copy-start | bytes 3145732
  426.9 6.4 %copy-start.7 = (bf16[8,256,256]{2,1,0:T(8,128)(2,1)S(1)}, bf16[8,256,256]{2,1,0:T(8,128)(2,1)}, u32[]{:S(2)}) copy-start(bf16[8,256,256]{2,1,0:T(8,128)(2,1)} %get-tuple-element.86) | copy-start | bytes 3145732
where the time goes:
time: 438 us; the launch traced here: 436 us
  waiting for transfers between devices  178 us (41%)
  local copies, waits for them, and re-layouts  107 us (24%)
  starting transfers between devices  57.3 us (13%)
  other arithmetic  36.2 us (8%)
  matrix products  33.6 us (8%)
  blocking collectives  23.4 us (5%)
    all_to_all x3, waiting for transfers between devices, shards(): lax.all_to_all(same_sent, 'lvl', split_axis=0, concat_axis=0, tiled=True)  139 us
    all_to_all x3, waiting for transfers between devices, shards(): lax.all_to_all(prior_sent, 'lvl', split_axis=0, concat_axis=0, tiled=True)  38.6 us
    gather x6, local copies, waits for them, and re-layouts, shards(): same_got.reshape(-1, block_rows, realize)  34.4 us
    all_to_all x3, starting transfers between devices, shards(): lax.all_to_all(prior_sent, 'lvl', split_axis=0, concat_axis=0, tiled=True)  30.1 us
    gather x6, local copies, waits for them, and re-layouts, fill_slots(): rows = held_blocks[jnp.maximum(picked, 0)]  29.1 us
    gather x6, local copies, waits for them, and re-layouts, shards(): crossed.reshape(-1, block_rows, realize)  28.3 us
    all_gather x1, blocking collectives, shards(): lax.all_gather(parents, 'lvl', axis=1, tiled=True)  23.4 us
    dot_general x3, matrix products, shards(): jnp.einsum('ksij,ksjr->kir', factors[section - 1], parent_vals, preferred...  21.6 us
  transfers between devices with their start and end apart: 10, of which 6 were waited for; matrix products, arithmetic and copies ran while one was open for 23% of the time, Pallas kernels for 0%

commit v1 on v0

v1 whole, which is shorter than its diff:
```python
import functools

import jax
import jax.numpy as jnp
from jax import lax
from jax.experimental import pallas as pl
from jax.experimental.pallas import tpu as pltpu
from jax.sharding import PartitionSpec as P

MESH = pl.DeviceIdType.MESH
NPAR = 4
CAP = 2
CAPX = 1
SLOTS = CAP + CAPX
SIDE = 4
FAR = (1, 3, 2)


def kernel(
    dims, req_ref, pos_ref, fac_ref, chol_ref, noise_ref, out_ref,
    held, got, cross, sent, passed, fac, low, draw, base, last,
    lists, table, g1s, g1r, g2s, g2r, hs, hr, xs, xr, fs, cs, cr,
    list_s, list_r, load_sem, out_sem, table_sem,
):
    depth, blocks, rows, half, tiles, span = dims
    tile = lax.axis_index("tile")
    lane = lax.axis_index("lvl")
    ix, iy = lane // SIDE, lane % SIDE

    def at(dx, dy):
        return ((ix + dx) % SIDE) * SIDE + (iy + dy) % SIDE

    def along(route, d):
        return {"lvl": at(d, 0) if route == 0 else at(0, d)}

    def across(route, d):
        return along(1 - route, d)

    def remote(src, dst, ssem, rsem, device):
        return pltpu.make_async_remote_copy(
            src_ref=src, dst_ref=dst, send_sem=ssem, recv_sem=rsem,
            device_id=device, device_id_type=MESH,
        )

    def arrived(ref, sem):
        remote(ref, ref, sem, sem, along(0, 1)).wait_recv()

    def gone(ref, sem):
        remote(ref, ref, sem, sem, along(0, 1)).wait_send()

    def load_level(level):
        p = level % 2
        return (
            pltpu.make_async_copy(chol_ref.at[level], low.at[p], load_sem.at[p]),
            pltpu.make_async_copy(noise_ref.at[level], draw.at[p], load_sem.at[2 + p]),
        )

    def load_factors(section):
        return pltpu.make_async_copy(fac_ref.at[section - 1], fac, load_sem.at[4])

    for level in (0, 1):
        for copy in load_level(level):
            copy.start()
    load_factors(1).start()

    barrier = pltpu.get_barrier_semaphore()
    for route in range(2):
        for d in FAR:
            pl.semaphore_signal(barrier, inc=1, device_id=across(route, d), device_id_type=MESH)

    @pl.when(tile > 0)
    def _():
        pl.semaphore_signal(barrier, inc=1, device_id={"tile": tile - 1}, device_id_type=MESH)

    @pl.when(tile < tiles - 1)
    def _():
        pl.semaphore_signal(barrier, inc=1, device_id={"tile": tile + 1}, device_id_type=MESH)

    ends = (tile > 0).astype(jnp.int32) + (tile < tiles - 1).astype(jnp.int32)
    pl.semaphore_wait(barrier, 6 + ends)

    @pl.when(tile > 0)
    def _():
        remote(
            req_ref, lists.at[1], list_s.at[0], list_r.at[0], {"tile": tile - 1}
        ).start()

    def peer(route, d):
        return 1 + 3 * route + FAR.index(d)

    def send_list(src, which):
        for route in range(2):
            for d in FAR:
                mine, theirs = peer(route, d), peer(route, SIDE - d)
                remote(
                    src, lists.at[2 * theirs + which], list_s.at[2 * mine + which],
                    list_r.at[2 * theirs + which], across(route, d),
                ).start()

    send_list(req_ref, 0)

    def spread(level, k):
        p = level % 2
        for route in range(2):
            for way, (d, o) in enumerate(((1, 1), (3, 3))):
                remote(
                    held[level][route][0].at[k], held[level][route][o].at[k],
                    g1s.at[p, route, way, k], g1r.at[p, route, way, k], along(route, d),
                ).start()

    def keep(level, k, total):
        value = total.astype(jnp.bfloat16)
        if level < depth - 1:
            held[level][0][0][k] = value[:, :half]
            held[level][1][0][k] = value[:, half:]

            @pl.when(k > 0)
            def _():
                spread(level, k - 1)
        else:
            last[k] = value

    def product(level, k):
        p = level % 2
        return jnp.dot(low[p, k], draw[p, k], preferred_element_type=jnp.float32)

    for copy in load_level(0):
        copy.wait()

    def first(k, carry):
        keep(0, k, product(0, k))
        return carry

    lax.fori_loop(0, blocks, first, 0)
    for copy in load_level(2):
        copy.start()
    spread(0, blocks - 1)

    lists[0] = req_ref[...]

    @pl.when(tile < tiles - 1)
    def _():
        arrived(lists.at[1], list_r.at[0])

    @pl.when(tile == tiles - 1)
    def _():
        lists[1] = req_ref[...]

    send_list(lists.at[1], 1)
    for route in range(2):
        for d in FAR:
            for which in range(2):
                n = 2 * peer(route, d) + which
                arrived(lists.at[n], list_r.at[n])
    copy = pltpu.make_async_copy(lists, table, table_sem)
    copy.start()
    copy.wait()

    def owner(route, o):
        column = at(-o, 0) if route == 0 else at(0, -o)
        return column * SLOTS

    def pick(section, route, o, wanted):
        within = wanted % blocks
        value = held[0][route][o][within]
        for level in range(1, section):
            value = jnp.where(
                wanted >= level * blocks, held[level][route][o][within], value
            )
        return value

    def wanted_at(section, n, route, o, slot):
        which = 0 if slot < CAP else 1
        return table[2 * n + which, section - 1, owner(route, o) + slot]

    def to_next(section, route, so, o, start):
        p = section % 2
        place = (so * SIDE + o) * SLOTS + CAP
        copy = remote(
            got[p][route].at[pl.ds(place, CAPX)],
            cross[section - 1][route].at[pl.ds(so * SIDE + o, CAPX)],
            cs.at[route, so, o], cr.at[section - 1, route, so, o], {"tile": tile + 1},
        )

        @pl.when(tile < tiles - 1)
        def _():
            if start:
                copy.start()
            else:
                copy.wait_send()

    PARTS = ((CAP, CAPX), (0, CAP))

    def hand(section, route, o, finish=False):
        p = section % 2
        for part, (begin, count) in enumerate(PARTS):
            for i, d in ((2, 2), (0, 1), (1, 3)):
                src = sent[route].at[pl.ds((i * SIDE + o) * SLOTS + begin, count)]
                if d == 2:
                    towards = 1 if o < 2 else 3
                    dst = passed[p][route].at[pl.ds(o * SLOTS + begin, count)]
                    rsem = xr.at[p, route, o, part]
                else:
                    towards = d
                    dst = got[p][route].at[pl.ds((d * SIDE + o) * SLOTS + begin, count)]
                    rsem = hr.at[p, route, d, o, part]
                copy = remote(src, dst, hs.at[route, i, o, part], rsem, across(route, towards))
                if finish:
                    copy.wait_send()
                else:
                    copy.start()

    def build(section, route, o):
        p = section % 2

        def one(i, carry):
            for slot in range(SLOTS):
                sent[route][(i * SIDE + o) * SLOTS + slot] = pick(
                    section, route, o, wanted_at(section, 1 + 3 * route + i, route, o, slot)
                )
            return carry

        lax.fori_loop(0, 3, one, 0)
        for slot in range(SLOTS):
            got[p][route][o * SLOTS + slot] = pick(
                section, route, o, wanted_at(section, 0, route, o, slot)
            )

    def relay(section, route, o, finish=False):
        p = section % 2
        towards = 1 if o < 2 else 3
        for part, (begin, count) in enumerate(PARTS):
            src = passed[p][route].at[pl.ds(o * SLOTS + begin, count)]
            copy = remote(
                src, got[p][route].at[pl.ds((2 * SIDE + o) * SLOTS + begin, count)],
                xs.at[route, o, part], hr.at[p, route, 2, o, part], across(route, towards),
            )
            if finish:
                copy.wait_send()
            else:
                arrived(src, xr.at[p, route, o, part])
                copy.start()

    def onward(section, route, so, o):
        p = section % 2
        place = (so * SIDE + o) * SLOTS + CAP
        arrived(got[p][route].at[pl.ds(place, CAPX)], hr.at[p, route, so, o, 0])
        to_next(section, route, so, o, True)

    def forward(level, k, start):
        p = level % 2
        for route in range(2):
            for way, (d, o) in enumerate(((1, 1), (3, 3))):
                block = 2 * k + way
                src = held[level][route][o].at[block]
                if start:
                    arrived(src, g1r.at[p, route, way, block])
                copy = remote(
                    src, held[level][route][2].at[block], g2s.at[p, route, way, k],
                    g2r.at[p, route, way, k], along(route, d),
                )
                if start:
                    copy.start()
                else:
                    copy.wait_send()

    def drain(section):
        for route in range(2):
            for o in range(SIDE):
                hand(section, route, o, finish=True)
                relay(section, route, o, finish=True)
                for so in range(SIDE):
                    to_next(section, route, so, o, False)

    def output(level):
        return [
            pltpu.make_async_copy(
                held[level][route][0],
                out_ref.at[level, :, :, pl.ds(route * half, half)],
                out_sem.at[2 * level + route],
            )
            for route in range(2)
        ]

    for section in range(1, depth):
        level = section - 1
        p = level % 2
        q = section % 2
        if section > 1:
            drain(section - 1)
        for route in range(2):
            build(section, route, 0)
            if route == 1:
                hand(section, 0, 0)
        hand(section, 1, 0)
        for route in range(2):
            to_next(section, route, 0, 0, True)

        for copy in load_level(section):
            copy.wait()

        def own(k, carry):
            base[k] = product(section, k)
            return carry

        lax.fori_loop(0, blocks, own, 0)
        if section + 2 < depth and section > 0:
            for copy in load_level(section + 2):
                copy.start()

        def pass_on(k, carry):
            forward(level, k, True)
            return carry

        lax.fori_loop(0, blocks // 2, pass_on, 0)

        def rest(k, carry):
            for route in range(2):
                arrived(held[level][route][1].at[2 * k + 1], g1r.at[p, route, 0, 2 * k + 1])
                arrived(held[level][route][3].at[2 * k], g1r.at[p, route, 1, 2 * k])
            return carry

        lax.fori_loop(0, blocks // 2, rest, 0)
        for o in (1, 3):
            for route in range(2):
                build(section, route, o)
            for route in range(2):
                hand(section, route, o)
                to_next(section, route, 0, o, True)
        for route in range(2):
            relay(section, route, 0)
        for route in range(2):
            for so in (1, 3):
                onward(section, route, so, 0)

        def second(k, carry):
            for route in range(2):
                for way in range(2):
                    arrived(
                        held[level][route][2].at[2 * k + way], g2r.at[p, route, way, k]
                    )
            return carry

        lax.fori_loop(0, blocks // 2, second, 0)
        for route in range(2):
            build(section, route, 2)
        for route in range(2):
            hand(section, route, 2)
            to_next(section, route, 0, 2, True)
        for o in (1, 3, 2):
            for route in range(2):
                relay(section, route, o)
        for copy in output(level):
            copy.start()
        for route in range(2):
            onward(section, route, 2, 0)
        for o in (1, 3, 2):
            for so in (1, 3, 2):
                for route in range(2):
                    onward(section, route, so, o)

        def sent_all(k, carry):
            for route in range(2):
                for way in range(2):
                    gone(held[level][route][0].at[k], g1s.at[p, route, way, k])
            return carry

        lax.fori_loop(0, blocks, sent_all, 0)

        def forwarded(k, carry):
            forward(level, k, False)
            return carry

        lax.fori_loop(0, blocks // 2, forwarded, 0)
        for route in range(2):
            for o in range(SIDE):
                for so in range(1, SIDE):
                    place = (so * SIDE + o) * SLOTS
                    arrived(got[q][route].at[pl.ds(place, CAP)], hr.at[q, route, so, o, 1])

        @pl.when(tile > 0)
        def _():
            for route in range(2):
                for o in range(SIDE):
                    for so in range(SIDE):
                        place = so * SIDE + o
                        arrived(
                            cross[section - 1][route].at[pl.ds(place, CAPX)],
                            cr.at[section - 1, route, so, o],
                        )

        load_factors(section).wait()

        def mix(k, carry):
            total = base[k]
            for slot in range(NPAR):
                code = pos_ref[section - 1, k * NPAR + slot]
                kind = code // 65536
                halves = []
                for route in range(2):
                    place = code % 256 if route == 0 else (code // 256) % 256
                    same = got[q][route][place % (SIDE * SIDE * SLOTS)]
                    prior = cross[section - 1][route][(place // SLOTS) % (SIDE * SIDE)]
                    value = jnp.where(kind == 2, prior, same)
                    halves.append(jnp.where(kind == 0, jnp.zeros_like(value), value))
                parent = jnp.concatenate(halves, axis=1)
                total = total + jnp.dot(
                    fac[k, slot], parent, preferred_element_type=jnp.float32
                )
            keep(section, k, total)
            if section == depth - 1:

                @pl.when(k > 0)
                def _():
                    write_last(k - 1).start()

            return carry

        def write_last(k):
            return pltpu.make_async_copy(
                last.at[k], out_ref.at[depth - 1, k], out_sem.at[2 * depth - 2 + k]
            )

        lax.fori_loop(0, blocks, mix, 0)
        if section < depth - 1:
            load_factors(section + 1).start()
            spread(section, blocks - 1)
        else:
            write_last(blocks - 1).start()

    drain(depth - 1)

    @pl.when(tile > 0)
    def _():
        gone(req_ref, list_s.at[0])

    for route in range(2):
        for d in FAR:
            for which in range(2):
                gone(req_ref, list_s.at[2 * peer(route, d) + which])
    for level in range(depth - 1):
        for copy in output(level):
            copy.wait()
    for k in range(blocks):
        pltpu.make_async_copy(
            last.at[k], out_ref.at[depth - 1, k], out_sem.at[2 * depth - 2 + k]
        ).wait()


def tables(parents, own_tile, lane, peers, blocks, total):
    sections = parents.shape[0]
    ids = parents.reshape(sections, -1)
    count = ids.shape[1]
    valid = ids >= 0
    ids = jnp.maximum(ids, 0)
    level, block = ids // total, ids % total
    device = block // blocks
    owner = device % peers
    prior = valid & (device // peers != own_tile)
    local = level * blocks + block % blocks
    group = jnp.where(valid, owner + peers * prior.astype(jnp.int32), -1)
    earlier = jnp.arange(count)[:, None] > jnp.arange(count)[None, :]
    rank = jnp.sum((group[:, :, None] == group[:, None, :]) & earlier, axis=2, dtype=jnp.int32)
    slot = jnp.where(prior, CAP, jnp.minimum(rank, CAP - 1))
    column = jnp.where(valid, owner * SLOTS + slot, -1)
    hits = column[:, None, :] == jnp.arange(128)[None, :, None]
    asked = jnp.sum(jnp.where(hits, local[:, None, :], 0), axis=2, dtype=jnp.int32)
    asked = jnp.concatenate([asked, jnp.zeros((8 - sections, 128), jnp.int32)])
    dx = (lane // SIDE - owner // SIDE) % SIDE
    dy = (lane % SIDE - owner % SIDE) % SIDE
    first = (dy * SIDE + dx) * SLOTS + slot
    second = (dx * SIDE + dy) * SLOTS + slot
    kind = jnp.where(valid, 1 + prior.astype(jnp.int32), 0)
    return asked, first + 256 * second + 65536 * kind


def shards(parents, factors, chol, noise):
    peers = lax.axis_size("lvl")
    tiles = lax.axis_size("tile")
    depth, blocks, rows, _ = chol.shape
    real = noise.shape[3]
    half = real // 2
    span = SIDE * SIDE
    asked, places = tables(
        parents, lax.axis_index("tile"), lax.axis_index("lvl"), peers, blocks,
        blocks * peers * tiles,
    )

    def vmem(*shape, dtype=jnp.bfloat16):
        return pltpu.VMEM(shape, dtype)

    dma = pltpu.SemaphoreType.DMA
    scratch = [
        [[[vmem(blocks, rows, half) for _ in range(SIDE)] for _ in range(2)] for _ in range(depth - 1)],
        [[vmem(span * SLOTS, rows, half) for _ in range(2)] for _ in range(2)],
        [[vmem(span, rows, half) for _ in range(2)] for _ in range(depth - 1)],
        [vmem(3 * SIDE * SLOTS, rows, half) for _ in range(2)],
        [[vmem(SIDE * SLOTS, rows, half) for _ in range(2)] for _ in range(2)],
        vmem(blocks, NPAR, rows, rows),
        vmem(2, blocks, rows, rows),
        vmem(2, blocks, rows, real),
        vmem(blocks, rows, real, dtype=jnp.float32),
        vmem(blocks, rows, real),
        vmem(14, 8, 128, dtype=jnp.int32),
        pltpu.SMEM((14, 8, 128), jnp.int32),
        dma((2, 2, 2, blocks)), dma((2, 2, 2, blocks)),
        dma((2, 2, 2, blocks // 2)), dma((2, 2, 2, blocks // 2)),
        dma((2, 3, SIDE, 2)), dma((2, 2, SIDE, SIDE, 2)),
        dma((2, SIDE, 2)), dma((2, 2, SIDE, 2)),
        dma((1,)),
        dma((2, SIDE, SIDE)), dma((depth - 1, 2, SIDE, SIDE)),
        dma((14,)), dma((14,)),
        dma((5,)), dma((2 * depth - 2 + blocks,)), dma,
    ]
    flat, tree = jax.tree.flatten(scratch)

    def body(*refs):
        operands, rest = refs[:6], refs[6:]
        kernel(
            (depth, blocks, rows, half, tiles, span), *operands,
            *jax.tree.unflatten(tree, rest),
        )

    anywhere = pl.BlockSpec(memory_space=pl.ANY)
    return pl.pallas_call(
        body,
        out_shape=jax.ShapeDtypeStruct((depth, blocks, rows, real), jnp.bfloat16),
        in_specs=[
            pl.BlockSpec(memory_space=pltpu.VMEM),
            pl.BlockSpec(memory_space=pltpu.SMEM),
            anywhere, anywhere, anywhere,
        ],
        out_specs=anywhere,
        scratch_shapes=flat,
        compiler_params=pltpu.CompilerParams(
            collective_id=0, has_side_effects=True, vmem_limit_bytes=67043328
        ),
        name="field",
    )(asked, places, factors, chol, noise)


def solution(mesh):
    placed = (
        P(None, ("tile", "lvl"), None),
        P(None, ("tile", "lvl"), None, None, None),
        P(None, ("tile", "lvl"), None, None),
        P(None, ("tile", "lvl"), None, None),
    )
    return jax.shard_map(
        shards,
        mesh=mesh,
        in_specs=placed,
        out_specs=P(None, ("tile", "lvl"), None, None),
        check_vma=False,
    )
```

time: 438 us -> 197 us (0.45)
  the two profiles are of different devices: /device:TPU:16 before, /device:TPU:32 now
where the time goes in v1:
time: 197 us
  Pallas kernels  188 us (95%)
  local copies, waits for them, and re-layouts  5.99 us (3%)
  other arithmetic  2.37 us (1%)
    pallas_call x1, Pallas kernels, shards(): pl.pallas_call(body, out_shape=jax.ShapeDtypeStruct((depth, blocks, rows,...  188 us
    unnamed x1, local copies, waits for them, and re-layouts  4.64 us

profile of v1, /device:TPU:32, one launch (start us, length us, event | category | flops | bytes accessed | tf_op | source)
XLA Modules:
  0.0 196.8 jit_solution(11239608754030047000)
XLA Ops:
  0.0 0.7 broadcast_compare_fusion
  0.7 0.1 copy.13
  0.8 0.1 ge.18
  0.9 0.1 copy.15
  1.0 0.1 ne.217
  1.1 0.7 maximum_and_fusion
  1.8 0.1 copy.14
  1.9 0.1 rem.126
  2.0 0.1 copy.16
  2.1 0.1 div.56
  2.2 0.2 convert_reduce_fusion
  2.4 0.6 multiply_add_fusion
  3.0 0.1 select_reduce_fusion
  3.1 0.6 concatenate.3.refs_0_
  3.7 188.4 %field.1 = bf16[4,8,256,256]{3,2,1,0:T(8,128)(2,1)} custom-call(s32[8,128]{1,0:T(8,128)} %concatenate.3.refs_0_, s32[3,32]{1,0:T(4,128)} %get-tuple-element.12.refs_1_, bf16[3,8,4,256,256]{4,3,2,1,0:T(8,128)(2,1)} %refs_2_.1, bf16[4,8,256,256]{3,2,1,0:T(8,128)(2,1)} %refs_3_.1, bf16[4,8,256,256]{3,2,1,0:T(8,128)(2,1)} %refs_4_.1), custom_call_target="tpu_custom_call" | custom-call | tf_op jit(solution)/shard_map/field/pallas_call | solution.py:525
  192.1 4.6 %copy.18 = bf16[4,8,256,256]{3,2,1,0:T(8,128)(2,1)} copy(bf16[4,8,256,256]{3,2,1,0:T(8,128)(2,1)} %field.1) | data formatting | bytes 8388608
  (2 shorter events, 0.0 us)

commit v2 on v0

v2 whole, which is shorter than its diff:
```python
import jax
import jax.numpy as jnp
from jax import lax
from jax.experimental import pallas as pl
from jax.experimental.pallas import tpu as pltpu
from jax.sharding import PartitionSpec as P

MESH = pl.DeviceIdType.MESH
NPAR = 4
CAP = 2
SIDE = 4
FAR = (2, 1, 3)
PIECES = 2


def kernel(
    dims, parents, fac_ref, chol_ref, noise_ref, out_ref,
    held, got, cross, sent_same, sent_next, fac, low, draw, base, last,
    asked, lists, table, codes, g1s, g1r, g2s, g2r, hs, hr, cs, cr,
    list_s, list_r, load_sem, out_sem, table_sem,
):
    depth, blocks, rows, real, tiles = dims
    tall, wide = rows // 2, real // 2
    piece = blocks // PIECES
    peers = SIDE * SIDE
    total_blocks = blocks * peers * tiles
    tile = lax.axis_index("tile")
    lane = lax.axis_index("lvl")
    ix, iy = lane // SIDE, lane % SIDE
    has_prior = tile > 0
    has_next = tile < tiles - 1

    def at(dx, dy):
        return ((ix + dx) % SIDE) * SIDE + (iy + dy) % SIDE

    def along(route, d):
        return at(d, 0) if route == 0 else at(0, d)

    def across(route, d):
        return along(1 - route, d)

    def remote(src, dst, ssem, rsem, device):
        return pltpu.make_async_remote_copy(
            src_ref=src, dst_ref=dst, send_sem=ssem, recv_sem=rsem,
            device_id=device, device_id_type=MESH,
        )

    def arrived(ref, sem):
        remote(ref, ref, sem, sem, {"lvl": at(1, 0)}).wait_recv()

    def load_level(level):
        p = level % 2
        return (
            pltpu.make_async_copy(chol_ref.at[level], low.at[p], load_sem.at[p]),
            pltpu.make_async_copy(noise_ref.at[level], draw.at[p], load_sem.at[2 + p]),
        )

    def load_factors(section):
        return pltpu.make_async_copy(fac_ref.at[section - 1], fac, load_sem.at[4])

    for level in (0, 1):
        for copy in load_level(level):
            copy.start()
    load_factors(1).start()

    barrier = pltpu.get_barrier_semaphore()

    def greet(device):
        pl.semaphore_signal(barrier, inc=1, device_id=device, device_id_type=MESH)

    for route in range(2):
        for d in FAR:
            greet({"lvl": across(route, d)})

    @pl.when(has_prior)
    def _():
        greet({"tile": tile - 1})
        for route in range(2):
            for d in FAR:
                greet({"tile": tile - 1, "lvl": across(route, d)})

    @pl.when(has_next)
    def _():
        greet({"tile": tile + 1})
        for route in range(2):
            for d in FAR:
                greet({"tile": tile + 1, "lvl": across(route, d)})

    def entry(section, n):
        number = parents[section - 1, n // NPAR, n % NPAR]
        clipped = jnp.maximum(number, 0)
        block = lax.rem(clipped, total_blocks)
        device = lax.div(block, blocks)
        local = lax.div(clipped, total_blocks) * blocks + lax.rem(block, blocks)
        return number >= 0, lax.div(device, peers) != tile, lax.rem(device, peers), local

    row = lax.broadcasted_iota(jnp.int32, (8, 128), 0)
    column = lax.broadcasted_iota(jnp.int32, (8, 128), 1)

    def ask(section):
        def one(n, carry):
            one_slot, two_slot, prior_slot = carry
            valid, prior, owner, local = entry(section, n)
            place = jnp.where(valid, jnp.where(prior, peers, 0) + owner, -1)
            here = (row == section - 1) & (column == place)
            there = (row == section - 1) & (column + peers == place) & (column < peers)
            here = here & (column < peers)
            two_slot = jnp.where(here & (one_slot >= 0), local, two_slot)
            one_slot = jnp.where(here & (one_slot < 0), local, one_slot)
            return one_slot, two_slot, jnp.where(there, local, prior_slot)

        return one

    state = (jnp.full((8, 128), -1, jnp.int32),) * 3
    for section in range(1, depth):
        state = lax.fori_loop(0, blocks * NPAR, ask(section), state)
    for slot in range(3):
        asked[slot] = jnp.maximum(state[slot], 0)

    ends = has_prior.astype(jnp.int32) + has_next.astype(jnp.int32)
    pl.semaphore_wait(barrier, 6 + 7 * ends)

    def peer(route, d):
        return 1 + 3 * route + FAR.index(d)

    def list_copies(which):
        moves = []
        if which == 1:
            moves.append((0, 0, {"tile": tile - 1}))
        for route in range(2):
            for d in FAR:
                device = {"lvl": across(route, d)}
                if which == 1:
                    device["tile"] = tile - 1
                moves.append((peer(route, d), peer(route, SIDE - d), device))
        return [
            remote(
                asked, lists.at[7 * which + theirs], list_s.at[7 * which + mine],
                list_r.at[7 * which + theirs], device,
            )
            for mine, theirs, device in moves
        ]

    for copy in list_copies(0):
        copy.start()

    @pl.when(has_prior)
    def _():
        for copy in list_copies(1):
            copy.start()

    WAYS = ((1, 1), (3, 3))

    def part(k):
        return pl.ds(k * piece, piece)

    def spread(level, chain, k):
        p = level % 2
        for route in range(2):
            own = held[level][chain][route]
            for way, (d, o) in enumerate(WAYS):
                remote(
                    own[0].at[part(k)], own[o].at[part(k)],
                    g1s.at[p, chain, route, way, k], g1r.at[p, chain, route, way, k],
                    {"lvl": along(route, d)},
                ).start()

    def forward(level, chain, start):
        p = level % 2
        for way, (d, o) in enumerate(WAYS):
            for route in range(2):
                own = held[level][chain][route]
                src = own[o].at[part(way)]
                if start:
                    arrived(src, g1r.at[p, chain, route, way, way])
                copy = remote(
                    src, own[2].at[part(way)], g2s.at[p, chain, route, way],
                    g2r.at[p, chain, route, way], {"lvl": along(route, d)},
                )
                if start:
                    copy.start()
                else:
                    copy.wait_send()

    def gathered(level, chain):
        p = level % 2
        for route in range(2):
            own = held[level][chain][route]
            for way, (d, o) in enumerate(WAYS):
                arrived(own[o].at[part(1 - way)], g1r.at[p, chain, route, way, 1 - way])
                arrived(own[2].at[part(way)], g2r.at[p, chain, route, way])

    def sent_on(level, chain):
        p = level % 2
        for route in range(2):
            own = held[level][chain][route]
            for way, (d, o) in enumerate(WAYS):
                for k in range(PIECES):
                    remote(
                        own[0].at[part(k)], own[0].at[part(k)],
                        g1s.at[p, chain, route, way, k], g1s.at[p, chain, route, way, k],
                        {"lvl": along(route, d)},
                    ).wait_send()
        forward(level, chain, False)

    def keep(level, chain, k, value):
        held[level][chain][0][0][k] = value[:tall]
        held[level][chain][1][0][k] = value[tall:]

    def product(level, k):
        p = level % 2
        return jnp.dot(low[p, k], draw[p, k], preferred_element_type=jnp.float32)

    for copy in load_level(0):
        copy.wait()

    def first(k, carry):
        value = product(0, k).astype(jnp.bfloat16)
        for chain in range(2):
            keep(0, chain, k, value[:, chain * wide : (chain + 1) * wide])
        return carry

    lax.fori_loop(0, piece, first, 0)
    spread(0, 0, 0)
    lax.fori_loop(piece, blocks, first, 0)
    for copy in load_level(2):
        copy.start()
    spread(0, 0, 1)
    for k in range(PIECES):
        spread(0, 1, k)

    def owner_lane(route, o):
        return at(-o, 0) if route == 0 else at(0, -o)

    def pick(section, chain, route, o, wanted):
        within = lax.rem(wanted, blocks)
        value = held[0][chain][route][o][within]
        for level in range(1, section):
            value = jnp.where(
                wanted >= level * blocks, held[level][chain][route][o][within], value
            )
        return value

    def build(section, chain, route):
        p = section % 2

        def one(i, carry):
            n = jnp.where(i == 3, 0, 1 + 3 * route + i)
            for o in range(SIDE):
                source = owner_lane(route, o)
                sent_next[chain][route][i * SIDE + o] = pick(
                    section, chain, route, o, table[7 + n, 2, section - 1, source]
                )
                for slot in range(CAP):
                    sent_same[chain][route][(i * SIDE + o) * CAP + slot] = pick(
                        section, chain, route, o, table[n, slot, section - 1, source]
                    )
            return carry

        lax.fori_loop(0, 3, one, 0)
        for o in range(SIDE):
            source = owner_lane(route, o)
            sent_next[chain][route][3 * SIDE + o] = pick(
                section, chain, route, o, table[7, 2, section - 1, source]
            )
            for slot in range(CAP):
                got[p][chain][route][o * CAP + slot] = pick(
                    section, chain, route, o, table[0, slot, section - 1, source]
                )

    def hand_next(section, chain, route, start):
        @pl.when(has_next)
        def _():
            for i, d in enumerate(FAR + (0,)):
                device = {"tile": tile + 1}
                if d:
                    device["lvl"] = across(route, d)
                copy = remote(
                    sent_next[chain][route].at[pl.ds(i * SIDE, SIDE)],
                    cross[section - 1][chain][route].at[pl.ds(d * SIDE, SIDE)],
                    cs.at[chain, route, d], cr.at[section - 1, chain, route, d], device,
                )
                if start:
                    copy.start()
                else:
                    copy.wait_send()

    def hand_same(section, chain, route, start):
        p = section % 2
        size = SIDE * CAP
        for i, d in enumerate(FAR):
            copy = remote(
                sent_same[chain][route].at[pl.ds(i * size, size)],
                got[p][chain][route].at[pl.ds(d * size, size)],
                hs.at[chain, route, d], hr.at[p, chain, route, d],
                {"lvl": across(route, d)},
            )
            if start:
                copy.start()
            else:
                copy.wait_send()

    def received(section, chain):
        p = section % 2
        size = SIDE * CAP
        for route in range(2):
            for d in FAR:
                arrived(
                    got[p][chain][route].at[pl.ds(d * size, size)], hr.at[p, chain, route, d]
                )

        @pl.when(has_prior)
        def _():
            for route in range(2):
                for d in range(SIDE):
                    arrived(
                        cross[section - 1][chain][route].at[pl.ds(d * SIDE, SIDE)],
                        cr.at[section - 1, chain, route, d],
                    )

    def output(level):
        return [
            pltpu.make_async_copy(
                held[level][chain][route][0],
                out_ref.at[level, :, pl.ds(route * tall, tall), pl.ds(chain * wide, wide)],
                out_sem.at[level, chain, route],
            )
            for chain in range(2)
            for route in range(2)
        ]

    def write_last(chain, k):
        columns = pl.ds(chain * wide, wide)
        return pltpu.make_async_copy(
            last.at[part(k), :, columns], out_ref.at[depth - 1, part(k), :, columns],
            out_sem.at[depth - 1, chain, k],
        )

    def mix(section, chain):
        p = section % 2

        def one(k, carry):
            total = base[k, :, chain * wide : (chain + 1) * wide]
            for slot in range(NPAR):
                code = codes[section - 1, k * NPAR + slot]
                kind = lax.div(code, 65536)
                halves = []
                for route in range(2):
                    place = lax.rem(code if route == 0 else lax.div(code, 256), 256)
                    same = got[p][chain][route][lax.rem(place, CAP * peers)]
                    prior = cross[section - 1][chain][route][lax.rem(lax.div(place, CAP), peers)]
                    value = jnp.where(kind == 2, prior, same)
                    halves.append(jnp.where(kind == 0, jnp.zeros_like(value), value))
                parent = jnp.concatenate(halves, axis=0)
                total = total + jnp.dot(
                    fac[k, slot], parent, preferred_element_type=jnp.float32
                )
            value = total.astype(jnp.bfloat16)
            if section < depth - 1:
                keep(section, chain, k, value)
            else:
                last[k, :, chain * wide : (chain + 1) * wide] = value
            return carry

        return one

    for section in range(1, depth):
        level = section - 1
        for chain in range(2):
            forward(level, chain, True)
        if section == 1:
            lists[0] = asked[...]
            for route in range(2):
                for d in FAR:
                    arrived(asked, list_r.at[peer(route, d)])

            @pl.when(has_next)
            def _():
                for n in range(7):
                    arrived(asked, list_r.at[7 + n])

            @pl.when(jnp.logical_not(has_next))
            def _():
                for n in range(7):
                    lists[7 + n] = asked[...]

            copy = pltpu.make_async_copy(lists, table, table_sem)
            copy.start()
            copy.wait()
        for chain in range(2):
            if section > 1:
                for route in range(2):
                    hand_next(section - 1, chain, route, False)
                    hand_same(section - 1, chain, route, False)
            gathered(level, chain)
            for route in range(2):
                build(section, chain, route)
                if route == 1:
                    for r in range(2):
                        hand_next(section, chain, r, True)
                    for r in range(2):
                        hand_same(section, chain, r, True)

        if section == 1:

            def encode(n, carry):
                for s in range(1, depth):
                    valid, prior, owner, local = entry(s, n)
                    dx = lax.rem(ix - lax.div(owner, SIDE) + SIDE, SIDE)
                    dy = lax.rem(iy - lax.rem(owner, SIDE) + SIDE, SIDE)
                    slot = jnp.where(table[0, 0, s - 1, owner] == local, 0, 1)
                    near = (dy * SIDE + dx) * CAP + slot
                    turned = (dx * SIDE + dy) * CAP + slot
                    kind = jnp.where(valid, jnp.where(prior, 2, 1), 0)
                    codes[s - 1, n] = near + 256 * turned + 65536 * kind
                return carry

            lax.fori_loop(0, blocks * NPAR, encode, 0)

        for copy in load_level(section):
            copy.wait()

        def own(k, carry):
            base[k] = product(section, k)
            return carry

        lax.fori_loop(0, blocks, own, 0)
        if section + 2 < depth:
            for copy in load_level(section + 2):
                copy.start()
        for copy in output(level):
            copy.start()
        for chain in range(2):
            sent_on(level, chain)
        load_factors(section).wait()
        for chain in range(2):
            received(section, chain)
            for k in range(PIECES):
                lax.fori_loop(k * piece, (k + 1) * piece, mix(section, chain), 0)
                if section < depth - 1:
                    spread(section, chain, k)
                else:
                    write_last(chain, k).start()
        if section < depth - 1:
            load_factors(section + 1).start()

    for chain in range(2):
        for route in range(2):
            hand_next(depth - 1, chain, route, False)
            hand_same(depth - 1, chain, route, False)
    for copy in list_copies(0):
        copy.wait_send()

    @pl.when(has_prior)
    def _():
        for copy in list_copies(1):
            copy.wait_send()

    for level in range(depth - 1):
        for copy in output(level):
            copy.wait()
    for chain in range(2):
        for k in range(PIECES):
            write_last(chain, k).wait()


def shards(parents, factors, chol, noise):
    tiles = lax.axis_size("tile")
    depth, blocks, rows, _ = chol.shape
    real = noise.shape[3]
    peers = SIDE * SIDE

    def vmem(*shape, dtype=jnp.bfloat16):
        return pltpu.VMEM(shape, dtype)

    def half(count):
        return vmem(count, rows // 2, real // 2)

    def pairs(make):
        return [[make() for _ in range(2)] for _ in range(2)]

    dma = pltpu.SemaphoreType.DMA
    scratch = [
        [pairs(lambda: [half(blocks) for _ in range(SIDE)]) for _ in range(depth - 1)],
        [pairs(lambda: half(peers * CAP)) for _ in range(2)],
        [pairs(lambda: half(peers)) for _ in range(depth - 1)],
        pairs(lambda: half(3 * SIDE * CAP)),
        pairs(lambda: half(4 * SIDE)),
        vmem(blocks, NPAR, rows, rows),
        vmem(2, blocks, rows, rows),
        vmem(2, blocks, rows, real),
        vmem(blocks, rows, real, dtype=jnp.float32),
        vmem(blocks, rows, real),
        vmem(3, 8, 128, dtype=jnp.int32),
        vmem(14, 3, 8, 128, dtype=jnp.int32),
        pltpu.SMEM((14, 3, 8, 128), jnp.int32),
        pltpu.SMEM((depth - 1, blocks * NPAR), jnp.int32),
        dma((2, 2, 2, 2, PIECES)), dma((2, 2, 2, 2, PIECES)),
        dma((2, 2, 2, 2)), dma((2, 2, 2, 2)),
        dma((2, 2, SIDE)), dma((2, 2, 2, SIDE)),
        dma((2, 2, SIDE)), dma((depth - 1, 2, 2, SIDE)),
        dma((14,)), dma((14,)),
        dma((5,)), dma((depth, 2, 2)), dma,
    ]
    flat, tree = jax.tree.flatten(scratch)

    def body(*refs):
        operands, rest = refs[:5], refs[5:]
        kernel(
            (depth, blocks, rows, real, tiles), *operands, *jax.tree.unflatten(tree, rest)
        )

    anywhere = pl.BlockSpec(memory_space=pl.ANY)
    return pl.pallas_call(
        body,
        out_shape=jax.ShapeDtypeStruct((depth, blocks, rows, real), jnp.bfloat16),
        in_specs=[pl.BlockSpec(memory_space=pltpu.SMEM), anywhere, anywhere, anywhere],
        out_specs=anywhere,
        scratch_shapes=flat,
        compiler_params=pltpu.CompilerParams(
            collective_id=0, has_side_effects=True, vmem_limit_bytes=67043328
        ),
        name="field",
    )(parents, factors, chol, noise)


def solution(mesh):
    placed = (
        P(None, ("tile", "lvl"), None),
        P(None, ("tile", "lvl"), None, None, None),
        P(None, ("tile", "lvl"), None, None),
        P(None, ("tile", "lvl"), None, None),
    )
    return jax.shard_map(
        shards,
        mesh=mesh,
        in_specs=placed,
        out_specs=P(None, ("tile", "lvl"), None, None),
        check_vma=False,
    )
```

time: 438 us -> 181 us (0.41)
  waiting for transfers between devices: 178 us -> 0 us
  Pallas kernels: 0 us -> 172 us
  local copies, waits for them, and re-layouts: 107 us -> 6.01 us
  starting transfers between devices: 57.3 us -> 0 us
  other arithmetic: 36.2 us -> 0 us
  matrix products: 33.6 us -> 0 us
  blocking collectives: 23.4 us -> 0 us
    all_to_all x6 -> x0, waiting for transfers between devices: 178 us -> none  [the longest x3 139 us: shards(): lax.all_to_all(same_sent, 'lvl', split_axis=0, concat_axis=0, tiled=True)]
    pallas_call x0 -> x1, Pallas kernels: none -> 172 us  [shards(): pl.pallas_call(body, out_shape=jax.ShapeDtypeStruct((depth, blocks, rows,...]
    gather x18 -> x0, local copies, waits for them, and re-layouts: 91.8 us -> none  [the longest x6 34.4 us: shards(): same_got.reshape(-1, block_rows, realize)]
    all_to_all x6 -> x0, starting transfers between devices: 51.5 us -> none  [the longest x3 30.1 us: shards(): lax.all_to_all(prior_sent, 'lvl', split_axis=0, concat_axis=0, tiled=True)]
    dot_general x7 -> x0, matrix products: 33.6 us -> none  [the longest x3 21.6 us: shards(): jnp.einsum('ksij,ksjr->kir', factors[section - 1], parent_vals, preferred...]
    all_gather x1 -> x0, blocking collectives: 23.4 us -> none  [shards(): lax.all_gather(parents, 'lvl', axis=1, tiled=True)]
    select_n x13 -> x0, other arithmetic: 19.2 us -> none  [the longest x6 19.1 us: fill_slots(): jnp.where((picked >= 0)[..., None, None], rows, jnp.zeros((), rows.dtype))]
    another operation x10 -> x0, other arithmetic: 8.71 us -> none  [the longest x9 6.41 us: decode(): before = jnp.cumsum(onehot, axis=-2) - onehot]
  transfers between devices with their start and end apart: 10 -> 0, of which waited for: 6 -> 0; matrix products, arithmetic and copies ran while one was open for 23% -> 0% of each run, Pallas kernels for 0% -> 0%
where the time goes in v2:
time: 181 us; the launch traced here: 178 us
  Pallas kernels  172 us (95%)
  local copies, waits for them, and re-layouts  6.01 us (3%)
    pallas_call x1, Pallas kernels, shards(): pl.pallas_call(body, out_shape=jax.ShapeDtypeStruct((depth, blocks, rows,...  172 us
    unnamed x2, local copies, waits for them, and re-layouts  6.01 us

profile of v2, /device:TPU:16, one launch (start us, length us, event | category | flops | bytes accessed | tf_op | source)
XLA Modules:
  0.0 177.7 jit_solution(3348388474263200186)
XLA Ops:
  0.0 1.4 copy.5.refs_0_
  1.4 171.6 %field.1 = bf16[4,8,256,256]{3,2,1,0:T(8,128)(2,1)} custom-call(s32[3,8,4]{2,1,0:T(8,128)} %copy.5.refs_0_, bf16[3,8,4,256,256]{4,3,2,1,0:T(8,128)(2,1)} %refs_1_.1, bf16[4,8,256,256]{3,2,1,0:T(8,128)(2,1)} %refs_2_.1, bf16[4,8,256,256]{3,2,1,0:T(8,128)(2,1)} %refs_3_.1), custom_call_target="tpu_custom_call" | custom-call | tf_op jit(solution)/shard_map/field/pallas_call | solution.py:514
  173.0 4.6 %copy.7 = bf16[4,8,256,256]{3,2,1,0:T(8,128)(2,1)} copy(bf16[4,8,256,256]{3,2,1,0:T(8,128)(2,1)} %field.1) | data formatting | bytes 8388608

commit v3 on v2

--- a/solution.py
+++ b/solution.py
@@ -15,14 +15,15 @@
 
 def kernel(
     dims, parents, fac_ref, chol_ref, noise_ref, out_ref,
-    held, got, cross, sent_same, sent_next, fac, low, draw, base, last,
-    asked, lists, table, codes, g1s, g1r, g2s, g2r, hs, hr, cs, cr,
+    held, got, cross, passed, sent_same, sent_next, fac, low, draw, base, last,
+    asked, lists, table, codes, g1s, g1r, g2s, g2r, hs, hr, cs, cr, ps, pr, qs, qr,
     list_s, list_r, load_sem, out_sem, table_sem,
 ):
     depth, blocks, rows, real, tiles = dims
     tall, wide = rows // 2, real // 2
     piece = blocks // PIECES
     peers = SIDE * SIDE
+    planes = tiles // 2
     total_blocks = blocks * peers * tiles
     tile = lax.axis_index("tile")
     lane = lax.axis_index("lvl")
@@ -58,10 +59,8 @@
     def load_factors(section):
         return pltpu.make_async_copy(fac_ref.at[section - 1], fac, load_sem.at[4])
 
-    for level in (0, 1):
-        for copy in load_level(level):
-            copy.start()
-    load_factors(1).start()
+    for copy in load_level(0):
+        copy.start()
 
     barrier = pltpu.get_barrier_semaphore()
 
@@ -87,7 +86,7 @@
                 greet({"tile": tile + 1, "lvl": across(route, d)})
 
     def entry(section, n):
-        number = parents[section - 1, n // NPAR, n % NPAR]
+        number = parents[section - 1, n % NPAR, n // NPAR]
         clipped = jnp.maximum(number, 0)
         block = lax.rem(clipped, total_blocks)
         device = lax.div(block, blocks)
@@ -213,6 +212,9 @@
 
     for copy in load_level(0):
         copy.wait()
+    for copy in load_level(1):
+        copy.start()
+    load_factors(1).start()
 
     def first(k, carry):
         value = product(0, k).astype(jnp.bfloat16)
@@ -220,9 +222,9 @@
             keep(0, chain, k, value[:, chain * wide : (chain + 1) * wide])
         return carry
 
-    lax.fori_loop(0, piece, first, 0)
+    lax.fori_loop(0, piece, first, 0, unroll=4)
     spread(0, 0, 0)
-    lax.fori_loop(piece, blocks, first, 0)
+    lax.fori_loop(piece, blocks, first, 0, unroll=4)
     for copy in load_level(2):
         copy.start()
     spread(0, 0, 1)
@@ -268,27 +270,82 @@
                     section, chain, route, o, table[0, slot, section - 1, source]
                 )
 
+    def share(plane):
+        return SIDE * (planes - 1 - plane) // planes
+
     def hand_next(section, chain, route, start):
-        @pl.when(has_next)
+        def act(copy):
+            if start:
+                copy.start()
+            else:
+                copy.wait_send()
+
+        def direct(i, d, count):
+            device = {"tile": tile + 1}
+            if d:
+                device["lvl"] = across(route, d)
+            act(
+                remote(
+                    sent_next[chain][route].at[pl.ds(i * SIDE, count)],
+                    cross[section - 1][chain][route].at[pl.ds(d * SIDE, count)],
+                    cs.at[chain, route, d], cr.at[section - 1, chain, route, d], device,
+                )
+            )
+
+        @pl.when(has_next & (tile % 2 == 0))
         def _():
             for i, d in enumerate(FAR + (0,)):
-                device = {"tile": tile + 1}
-                if d:
-                    device["lvl"] = across(route, d)
-                copy = remote(
-                    sent_next[chain][route].at[pl.ds(i * SIDE, SIDE)],
-                    cross[section - 1][chain][route].at[pl.ds(d * SIDE, SIDE)],
-                    cs.at[chain, route, d], cr.at[section - 1, chain, route, d], device,
-                )
-                if start:
-                    copy.start()
-                else:
-                    copy.wait_send()
-
-    def hand_same(section, chain, route, start):
+                direct(i, d, SIDE)
+
+        for plane in range(planes - 1):
+
+            @pl.when(tile == 2 * plane + 1)
+            def _():
+                count = share(plane)
+                for i, d in enumerate(FAR):
+                    place = pl.ds(i * SIDE + count, SIDE - count)
+                    act(
+                        remote(
+                            sent_next[chain][route].at[place],
+                            passed[section - 1][chain][route].at[place],
+                            ps.at[chain, route, d], pr.at[section - 1, chain, route, d],
+                            {"tile": tile + 1},
+                        )
+                    )
+                for i, d in enumerate(FAR + (0,)):
+                    direct(i, d, count if d else SIDE)
+
+    def pass_next(section, chain, start):
+        for plane in range(planes - 1):
+
+            @pl.when(tile == 2 * plane + 2)
+            def _():
+                count = share(plane)
+                for i, d in enumerate(FAR):
+                    for route in range(2):
+                        src = passed[section - 1][chain][route].at[
+                            pl.ds(i * SIDE + count, SIDE - count)
+                        ]
+                        if start:
+                            arrived(src, pr.at[section - 1, chain, route, d])
+                        copy = remote(
+                            src,
+                            cross[section - 1][chain][route].at[
+                                pl.ds(d * SIDE + count, SIDE - count)
+                            ],
+                            qs.at[chain, route, d], qr.at[section - 1, chain, route, d],
+                            {"lvl": across(route, d)},
+                        )
+                        if start:
+                            copy.start()
+                        else:
+                            copy.wait_send()
+
+    def hand_same(section, chain, route, start, readers=FAR):
         p = section % 2
         size = SIDE * CAP
-        for i, d in enumerate(FAR):
+        for d in readers:
+            i = FAR.index(d)
             copy = remote(
                 sent_same[chain][route].at[pl.ds(i * size, size)],
                 got[p][chain][route].at[pl.ds(d * size, size)],
@@ -309,14 +366,27 @@
                     got[p][chain][route].at[pl.ds(d * size, size)], hr.at[p, chain, route, d]
                 )
 
-        @pl.when(has_prior)
+        def prior(d, begin, count, sems):
+            for route in range(2):
+                arrived(
+                    cross[section - 1][chain][route].at[pl.ds(d * SIDE + begin, count)],
+                    sems.at[section - 1, chain, route, d],
+                )
+
+        @pl.when(tile % 2 == 1)
         def _():
-            for route in range(2):
-                for d in range(SIDE):
-                    arrived(
-                        cross[section - 1][chain][route].at[pl.ds(d * SIDE, SIDE)],
-                        cr.at[section - 1, chain, route, d],
-                    )
+            for d in range(SIDE):
+                prior(d, 0, SIDE, cr)
+
+        for plane in range(planes - 1):
+
+            @pl.when(tile == 2 * plane + 2)
+            def _():
+                count = share(plane)
+                prior(0, 0, SIDE, cr)
+                for d in FAR:
+                    prior(d, 0, count, cr)
+                    prior(d, count, SIDE - count, qr)
 
     def output(level):
         return [
@@ -392,14 +462,21 @@
                 for route in range(2):
                     hand_next(section - 1, chain, route, False)
                     hand_same(section - 1, chain, route, False)
+                pass_next(section - 1, chain, False)
             gathered(level, chain)
             for route in range(2):
                 build(section, chain, route)
-                if route == 1:
-                    for r in range(2):
-                        hand_next(section, chain, r, True)
-                    for r in range(2):
-                        hand_same(section, chain, r, True)
+            for route in range(2):
+                hand_next(section, chain, route, True)
+            if chain == 0:
+                for route in range(2):
+                    hand_same(section, 0, route, True, FAR[:1])
+        pass_next(section, 0, True)
+        for route in range(2):
+            hand_same(section, 0, route, True, FAR[1:])
+        pass_next(section, 1, True)
+        for route in range(2):
+            hand_same(section, 1, route, True)
 
         if section == 1:
 
@@ -424,7 +501,7 @@
             base[k] = product(section, k)
             return carry
 
-        lax.fori_loop(0, blocks, own, 0)
+        lax.fori_loop(0, blocks, own, 0, unroll=4)
         if section + 2 < depth:
             for copy in load_level(section + 2):
                 copy.start()
@@ -436,7 +513,7 @@
         for chain in range(2):
             received(section, chain)
             for k in range(PIECES):
-                lax.fori_loop(k * piece, (k + 1) * piece, mix(section, chain), 0)
+                lax.fori_loop(k * piece, (k + 1) * piece, mix(section, chain), 0, unroll=2)
                 if section < depth - 1:
                     spread(section, chain, k)
                 else:
@@ -448,6 +525,7 @@
         for route in range(2):
             hand_next(depth - 1, chain, route, False)
             hand_same(depth - 1, chain, route, False)
+        pass_next(depth - 1, chain, False)
     for copy in list_copies(0):
         copy.wait_send()
 
@@ -464,6 +542,30 @@
             write_last(chain, k).wait()
 
 
+def settle(src, dst, hold, in_sem, out_sem):
+    depth, blocks = src.shape[:2]
+    parts = [
+        (level, k, pl.ds(k * (blocks // PIECES), blocks // PIECES))
+        for level in range(depth)
+        for k in range(PIECES)
+    ]
+    for level, k, part in parts:
+        pltpu.make_async_copy(
+            src.at[level, part], hold.at[level, part], in_sem.at[level, k]
+        ).start()
+    for level, k, part in parts:
+        pltpu.make_async_copy(
+            src.at[level, part], hold.at[level, part], in_sem.at[level, k]
+        ).wait()
+        pltpu.make_async_copy(
+            hold.at[level, part], dst.at[level, part], out_sem.at[level, k]
+        ).start()
+    for level, k, part in parts:
+        pltpu.make_async_copy(
+            hold.at[level, part], dst.at[level, part], out_sem.at[level, k]
+        ).wait()
+
+
 def shards(parents, factors, chol, noise):
     tiles = lax.axis_size("tile")
     depth, blocks, rows, _ = chol.shape
@@ -484,6 +586,7 @@
         [pairs(lambda: [half(blocks) for _ in range(SIDE)]) for _ in range(depth - 1)],
         [pairs(lambda: half(peers * CAP)) for _ in range(2)],
         [pairs(lambda: half(peers)) for _ in range(depth - 1)],
+        [pairs(lambda: half(3 * SIDE)) for _ in range(depth - 1)],
         pairs(lambda: half(3 * SIDE * CAP)),
         pairs(lambda: half(4 * SIDE)),
         vmem(blocks, NPAR, rows, rows),
@@ -499,6 +602,8 @@
         dma((2, 2, 2, 2)), dma((2, 2, 2, 2)),
         dma((2, 2, SIDE)), dma((2, 2, 2, SIDE)),
         dma((2, 2, SIDE)), dma((depth - 1, 2, 2, SIDE)),
+        dma((2, 2, SIDE)), dma((depth - 1, 2, 2, SIDE)),
+        dma((2, 2, SIDE)), dma((depth - 1, 2, 2, SIDE)),
         dma((14,)), dma((14,)),
         dma((5,)), dma((depth, 2, 2)), dma,
     ]
@@ -511,7 +616,7 @@
         )
 
     anywhere = pl.BlockSpec(memory_space=pl.ANY)
-    return pl.pallas_call(
+    field = pl.pallas_call(
         body,
         out_shape=jax.ShapeDtypeStruct((depth, blocks, rows, real), jnp.bfloat16),
         in_specs=[pl.BlockSpec(memory_space=pltpu.SMEM), anywhere, anywhere, anywhere],
@@ -521,7 +626,17 @@
             collective_id=0, has_side_effects=True, vmem_limit_bytes=67043328
         ),
         name="field",
-    )(parents, factors, chol, noise)
+    )(parents.transpose(0, 2, 1), factors, chol, noise)
+    return pl.pallas_call(
+        settle,
+        out_shape=jax.ShapeDtypeStruct(field.shape, field.dtype),
+        in_specs=[anywhere],
+        out_specs=anywhere,
+        scratch_shapes=[
+            vmem(*field.shape), dma((depth, PIECES)), dma((depth, PIECES)),
+        ],
+        name="settle",
+    )(field)
 
 
 def solution(mesh):

time: 181 us -> 170 us (0.939)
  local copies, waits for them, and re-layouts: 6.01 us -> 0 us
  Pallas kernels: 172 us -> 168 us
    pallas_call x1, Pallas kernels: 172 us -> 164 us  [shards(): pl.pallas_call(body, out_shape=jax.ShapeDtypeStruct((depth, blocks, rows,...]
    unnamed x2 -> x0, local copies, waits for them, and re-layouts: 6.01 us -> none
    pallas_call x0 -> x1, Pallas kernels: none -> 3.58 us  [shards(): pl.pallas_call(settle, out_shape=jax.ShapeDtypeStruct(field.shape, field....]
where the time goes in v3:
time: 170 us; the launch traced here: 168 us
  Pallas kernels  168 us (99%)
    pallas_call x1, Pallas kernels, shards(): pl.pallas_call(body, out_shape=jax.ShapeDtypeStruct((depth, blocks, rows,...  164 us
    pallas_call x1, Pallas kernels, shards(): pl.pallas_call(settle, out_shape=jax.ShapeDtypeStruct(field.shape, field....  3.58 us

profile of v3, /device:TPU:16, one launch (start us, length us, event | category | flops | bytes accessed | tf_op | source)
XLA Modules:
  0.0 168.2 jit_solution(8922416499795540219)
XLA Ops:
  0.0 164.4 %field.1.src = bf16[4,8,256,256]{3,2,1,0:T(8,128)(2,1)} custom-call(s32[3,4,8]{2,1,0:T(4,128)} %bitcast.1, bf16[3,8,4,256,256]{4,3,2,1,0:T(8,128)(2,1)} %refs_1_.1, bf16[4,8,256,256]{3,2,1,0:T(8,128)(2,1)} %refs_2_.1, bf16[4,8,256,256]{3,2,1,0:T(8,128)(2,1)} %refs_3_.1), custom_call_target="tpu_custom_call" | custom-call | tf_op jit(solution)/shard_map/field/pallas_call | solution.py:619
  164.4 3.6 %settle.1 = bf16[4,8,256,256]{3,2,1,0:T(8,128)(2,1)} custom-call(bf16[4,8,256,256]{3,2,1,0:T(8,128)(2,1)} %field.1.src), custom_call_target="tpu_custom_call" | custom-call | tf_op jit(solution)/shard_map/settle/pallas_call | solution.py:630

commit v4 on v3

--- a/solution.py
+++ b/solution.py
@@ -85,6 +85,17 @@
             for d in FAR:
                 greet({"tile": tile + 1, "lvl": across(route, d)})
 
+    odd = tile % 2 == 1
+    skips_back, skips_on = odd & (tile > 1), odd & (tile < tiles - 1)
+
+    @pl.when(skips_back)
+    def _():
+        greet({"tile": tile - 2})
+
+    @pl.when(skips_on)
+    def _():
+        greet({"tile": tile + 2})
+
     def entry(section, n):
         number = parents[section - 1, n % NPAR, n // NPAR]
         clipped = jnp.maximum(number, 0)
@@ -117,7 +128,8 @@
         asked[slot] = jnp.maximum(state[slot], 0)
 
     ends = has_prior.astype(jnp.int32) + has_next.astype(jnp.int32)
-    pl.semaphore_wait(barrier, 6 + 7 * ends)
+    skips = skips_back.astype(jnp.int32) + skips_on.astype(jnp.int32)
+    pl.semaphore_wait(barrier, 6 + 7 * ends + skips)
 
     def peer(route, d):
         return 1 + 3 * route + FAR.index(d)
@@ -270,8 +282,9 @@
                     section, chain, route, o, table[0, slot, section - 1, source]
                 )
 
-    def share(plane):
-        return SIDE * (planes - 1 - plane) // planes
+    def share(plane, section):
+        count = SIDE * (planes - 1 - plane) // planes
+        return count - 1 if section == depth - 1 and count > 1 else count
 
     def hand_next(section, chain, route, start):
         def act(copy):
@@ -301,7 +314,7 @@
 
             @pl.when(tile == 2 * plane + 1)
             def _():
-                count = share(plane)
+                count = share(plane, section)
                 for i, d in enumerate(FAR):
                     place = pl.ds(i * SIDE + count, SIDE - count)
                     act(
@@ -309,7 +322,7 @@
                             sent_next[chain][route].at[place],
                             passed[section - 1][chain][route].at[place],
                             ps.at[chain, route, d], pr.at[section - 1, chain, route, d],
-                            {"tile": tile + 1},
+                            {"tile": tile + 2},
                         )
                     )
                 for i, d in enumerate(FAR + (0,)):
@@ -318,9 +331,9 @@
     def pass_next(section, chain, start):
         for plane in range(planes - 1):
 
-            @pl.when(tile == 2 * plane + 2)
+            @pl.when(tile == 2 * plane + 3)
             def _():
-                count = share(plane)
+                count = share(plane, section)
                 for i, d in enumerate(FAR):
                     for route in range(2):
                         src = passed[section - 1][chain][route].at[
@@ -334,7 +347,7 @@
                                 pl.ds(d * SIDE + count, SIDE - count)
                             ],
                             qs.at[chain, route, d], qr.at[section - 1, chain, route, d],
-                            {"lvl": across(route, d)},
+                            {"tile": tile - 1, "lvl": across(route, d)},
                         )
                         if start:
                             copy.start()
@@ -382,7 +395,7 @@
 
             @pl.when(tile == 2 * plane + 2)
             def _():
-                count = share(plane)
+                count = share(plane, section)
                 prior(0, 0, SIDE, cr)
                 for d in FAR:
                     prior(d, 0, count, cr)

time: 170 us -> 169 us (level)
  no operation moved by 1% of the time
where the time goes in v4:
time: 169 us; the launch traced here: 167 us
  Pallas kernels  167 us (99%)
    pallas_call x1, Pallas kernels, shards(): pl.pallas_call(body, out_shape=jax.ShapeDtypeStruct((depth, blocks, rows,...  163 us
    pallas_call x1, Pallas kernels, shards(): pl.pallas_call(settle, out_shape=jax.ShapeDtypeStruct(field.shape, field....  3.58 us

profile of v4, /device:TPU:16, one launch (start us, length us, event | category | flops | bytes accessed | tf_op | source)
XLA Modules:
  0.0 166.8 jit_solution(16247574594180267248)
XLA Ops:
  0.0 163.1 %field.1.src = bf16[4,8,256,256]{3,2,1,0:T(8,128)(2,1)} custom-call(s32[3,4,8]{2,1,0:T(4,128)} %bitcast.1, bf16[3,8,4,256,256]{4,3,2,1,0:T(8,128)(2,1)} %refs_1_.1, bf16[4,8,256,256]{3,2,1,0:T(8,128)(2,1)} %refs_2_.1, bf16[4,8,256,256]{3,2,1,0:T(8,128)(2,1)} %refs_3_.1), custom_call_target="tpu_custom_call" | custom-call | tf_op jit(solution)/shard_map/field/pallas_call | solution.py:632
  163.1 3.6 %settle.1 = bf16[4,8,256,256]{3,2,1,0:T(8,128)(2,1)} custom-call(bf16[4,8,256,256]{3,2,1,0:T(8,128)(2,1)} %field.1.src), custom_call_target="tpu_custom_call" | custom-call | tf_op jit(solution)/shard_map/settle/pallas_call | solution.py:643

commit v5 on v4

--- a/solution.py
+++ b/solution.py
@@ -526,7 +526,7 @@
         for chain in range(2):
             received(section, chain)
             for k in range(PIECES):
-                lax.fori_loop(k * piece, (k + 1) * piece, mix(section, chain), 0, unroll=2)
+                lax.fori_loop(k * piece, (k + 1) * piece, mix(section, chain), 0, unroll=4)
                 if section < depth - 1:
                     spread(section, chain, k)
                 else:
@@ -558,9 +558,9 @@
 def settle(src, dst, hold, in_sem, out_sem):
     depth, blocks = src.shape[:2]
     parts = [
-        (level, k, pl.ds(k * (blocks // PIECES), blocks // PIECES))
+        (level, k, pl.ds(k * (blocks // 4), blocks // 4))
         for level in range(depth)
-        for k in range(PIECES)
+        for k in range(4)
     ]
     for level, k, part in parts:
         pltpu.make_async_copy(
@@ -646,7 +646,7 @@
         in_specs=[anywhere],
         out_specs=anywhere,
         scratch_shapes=[
-            vmem(*field.shape), dma((depth, PIECES)), dma((depth, PIECES)),
+            vmem(*field.shape), dma((depth, 4)), dma((depth, 4)),
         ],
         name="settle",
     )(field)

time: 169 us -> 169 us (level)
  no operation moved by 1% of the time
where the time goes in v5:
time: 169 us; the launch traced here: 167 us
  Pallas kernels  166 us (98%)
    pallas_call x1, Pallas kernels, shards(): pl.pallas_call(body, out_shape=jax.ShapeDtypeStruct((depth, blocks, rows,...  163 us
    pallas_call x1, Pallas kernels, shards(): pl.pallas_call(settle, out_shape=jax.ShapeDtypeStruct(field.shape, field....  3.85 us

profile of v5, /device:TPU:16, one launch (start us, length us, event | category | flops | bytes accessed | tf_op | source)
XLA Modules:
  0.0 166.6 jit_solution(9352256191740755253)
XLA Ops:
  0.0 162.5 %field.1.src = bf16[4,8,256,256]{3,2,1,0:T(8,128)(2,1)} custom-call(s32[3,4,8]{2,1,0:T(4,128)} %bitcast.1, bf16[3,8,4,256,256]{4,3,2,1,0:T(8,128)(2,1)} %refs_1_.1, bf16[4,8,256,256]{3,2,1,0:T(8,128)(2,1)} %refs_2_.1, bf16[4,8,256,256]{3,2,1,0:T(8,128)(2,1)} %refs_3_.1), custom_call_target="tpu_custom_call" | custom-call | tf_op jit(solution)/shard_map/field/pallas_call | solution.py:632
  162.6 3.9 %settle.1 = bf16[4,8,256,256]{3,2,1,0:T(8,128)(2,1)} custom-call(bf16[4,8,256,256]{3,2,1,0:T(8,128)(2,1)} %field.1.src), custom_call_target="tpu_custom_call" | custom-call | tf_op jit(solution)/shard_map/settle/pallas_call | solution.py:643
